TPU v7x, 32 devices: a whole 2x2x4 slice. The times are simulated.
32 devices in a mesh: state: 4 (over z), basis: 8 (over y, x, core).
Axes of the slice: x: 2, y: 2, z: 4, core: 2. Of those that a mesh axis runs over, the one named last changes fastest.
Arguments:
- states: float32 [8, 64, 64000], P('state', 'basis'), may hold values from -40 to 40
- membrane_step: float32 [40, 40], replicated, may hold values from -1 to 1
- cavity_forward: float32 [64, 64], replicated, may hold values from -0.75 to 0.75
- coupling: float32 [64, 40], replicated, may hold values from 0.25 to 1
- membrane_forward: float32 [40, 40], replicated, may hold values from -1 to 1
- cavity_back: float32 [64, 64], replicated, may hold values from -9 to 9
- membrane_back: float32 [40, 40], replicated, may hold values from -1 to 1
Outputs:
- orthonormal: float32 [8, 64, 64000], P('state', 'basis')
All inputs are finite; a program needn't handle non-finite values.
Results may differ from a plain program's by a relative error of at most 0.000075.
Values sent between devices are 32-bit elements; how exact they have to be, the bound alone decides.
A program may use at most 192 MiB of HBM per device.

v0:
```python
import functools

import jax
import jax.numpy as jnp
from jax import lax
from jax.experimental import pallas as pl
from jax.experimental.pallas import tpu as pltpu
from jax.sharding import PartitionSpec as P

LANES = 128
GROUP_BLOCKS = 16
VMEM_LIMIT = 60 * 1024 * 1024


def plain_body(
    states, membrane_step, cavity_forward, coupling, membrane_forward, cavity_back, membrane_back
):
    highest = lax.Precision.HIGHEST
    panel_size, level_count, joint = states.shape
    levels_all = cavity_forward.shape[0]
    membrane_levels = membrane_step.shape[0]
    basis_total = float(levels_all * joint)
    head = jnp.einsum(
        "ab,scbr->scar",
        membrane_step,
        states.reshape(panel_size, level_count, membrane_levels, joint // membrane_levels),
        precision=highest,
    )
    head = head.reshape(panel_size, level_count, joint)
    panel_block = lax.all_to_all(head, "basis", split_axis=2, concat_axis=1, tiled=True)
    items, cavity_all, columns = panel_block.shape
    grid = jnp.einsum("qc,kcr->kqr", cavity_forward, panel_block, precision=highest)
    grid = jnp.einsum(
        "kqtm,nm->kqtn",
        grid.reshape(items, cavity_all, columns // membrane_levels, membrane_levels),
        membrane_forward,
        precision=highest,
    )
    weighted = grid * coupling[None, :, None, :]
    backward = jnp.einsum("kqtn,mn->kqtm", weighted, membrane_back, precision=highest)
    backward = backward.reshape(items, cavity_all, columns)
    stepped = jnp.einsum("cq,kqr->kcr", cavity_back, backward, precision=highest)
    spread = lax.all_to_all(stepped, "state", split_axis=2, concat_axis=0, tiled=True)
    state_total, spread_levels, spread_cols = spread.shape
    flattened = spread.reshape(state_total, -1)
    partial_gram = jnp.dot(flattened, flattened.T, precision=highest)
    gram = lax.psum(partial_gram, ("state", "basis")) / basis_total
    lower_factor = jnp.linalg.cholesky(gram)
    identity = jnp.eye(state_total, dtype=gram.dtype)
    inverse = lax.linalg.triangular_solve(lower_factor, identity, left_side=True, lower=True)
    local_result = jnp.dot(inverse, flattened, precision=highest)
    local_result = local_result.reshape(state_total, spread_levels, spread_cols)
    return lax.all_to_all(
        lax.all_to_all(local_result, "state", split_axis=0, concat_axis=2, tiled=True),
        "basis",
        split_axis=1,
        concat_axis=2,
        tiled=True,
    )


def split2(x):
    hi = x.astype(jnp.bfloat16)
    lo = (x - hi.astype(jnp.float32)).astype(jnp.bfloat16)
    return hi, lo


def bdot(a, b):
    return jnp.dot(a, b, preferred_element_type=jnp.float32)


def left3(wh, wl, x):
    xh, xl = split2(x)
    return bdot(jnp.concatenate([wh, wl, wh], axis=1), jnp.concatenate([xh, xh, xl], axis=0))


def right3(x, wh, wl):
    xh, xl = split2(x)
    return bdot(xh, wh) + bdot(xl, wh) + bdot(xh, wl)


def kron_left(w, reps, out_ref_h, out_ref_l):
    m = w.shape[0]
    n = m * reps
    row = lax.broadcasted_iota(jnp.int32, (n, m), 0)
    col = lax.broadcasted_iota(jnp.int32, (n, m), 1)
    left = (row // reps == col).astype(jnp.bfloat16)
    right_row = lax.broadcasted_iota(jnp.int32, (m, n), 0)
    right_col = lax.broadcasted_iota(jnp.int32, (m, n), 1)
    right = (right_col // reps == right_row).astype(jnp.bfloat16)
    a = lax.broadcasted_iota(jnp.int32, (n, 1), 0)
    b = lax.broadcasted_iota(jnp.int32, (1, n), 1)
    keep = lax.rem(a, reps) == lax.rem(b, reps)
    for part, ref in zip(split2(w), (out_ref_h, out_ref_l)):
        full = bdot(bdot(left, part).astype(jnp.bfloat16), right)
        ref[...] = jnp.where(keep, full, 0.0).astype(jnp.bfloat16)


def kron_lanes(w_t, reps, out_ref_h, out_ref_l):
    m = w_t.shape[0]
    n = m * reps
    left = (
        lax.rem(lax.broadcasted_iota(jnp.int32, (n, m), 0), m)
        == lax.broadcasted_iota(jnp.int32, (n, m), 1)
    ).astype(jnp.bfloat16)
    right = (
        lax.rem(lax.broadcasted_iota(jnp.int32, (m, n), 1), m)
        == lax.broadcasted_iota(jnp.int32, (m, n), 0)
    ).astype(jnp.bfloat16)
    a = lax.broadcasted_iota(jnp.int32, (n, 1), 0)
    b = lax.broadcasted_iota(jnp.int32, (1, n), 1)
    keep = a // m == b // m
    for part, ref in zip(split2(w_t), (out_ref_h, out_ref_l)):
        full = bdot(bdot(left, part).astype(jnp.bfloat16), right)
        ref[...] = jnp.where(keep, full, 0.0).astype(jnp.bfloat16)


def remote(src, dst, send_sem, recv_sem, axis, peer):
    return pltpu.make_async_remote_copy(
        src_ref=src,
        dst_ref=dst,
        send_sem=send_sem,
        recv_sem=recv_sem,
        device_id={axis: peer},
        device_id_type=pl.DeviceIdType.MESH,
    )


def peers_of(axis, size):
    me = lax.axis_index(axis)
    return me, [lax.rem(me + d, size) for d in range(1, size)]


def state_peers(size):
    me = lax.axis_index("state")
    if size != 4:
        return peers_of("state", size)
    near = 3 - 2 * lax.rem(me, 2)
    return me, [lax.rem(me + d, size) for d in (2, near, 4 - near)]


def bulk_tiles(x_ref, q, h, low, nz, ns):
    width = x_ref.shape[-1]
    bulk = (width - LANES) // ns
    for t in range(bulk // LANES):
        yield t, [
            x_ref[q, a // ns, h, :, (a % ns) * bulk + t * LANES : (a % ns) * bulk + (t + 1) * LANES]
            for a in range(nz * ns)
        ]
    vals = []
    for z in range(nz):
        v = x_ref[q, z, h, :, width - LANES :]
        vals += [jnp.where(low, v, 0.0), jnp.where(low, pltpu.roll(v, LANES // 2, 1), 0.0)]
    yield None, vals


def step_kernel(
    nz,
    nb,
    x_ref,
    ms_ref,
    fc_ref,
    cp_ref,
    fk_ref,
    bc_ref,
    bk_ref,
    o_ref,
    xin,
    kh,
    kl,
    xs,
    outgo,
    fh,
    fl,
    bh,
    bl,
    cps,
    work,
    block,
    stepped,
    spread,
    gram_b,
    gram_z,
    splat,
    mixed,
    held,
    home,
    in_sem,
    b_send,
    b_recv,
    z_send,
    z_recv,
    gb_send,
    gb_recv,
    gz_send,
    gz_recv,
    y_send,
    y_recv,
    c_send,
    c_recv,
):
    _, nq, ns, lev, width = outgo.shape
    half = nb // nz
    total = nz * ns
    c_all = fc_ref.shape[0]
    m = fk_ref.shape[0]
    cols = x_ref.shape[2] // m
    group = m * GROUP_BLOCKS
    packed = ns * cols
    bulk = (packed - LANES) // ns
    pieces = [pl.ds(0, bulk), pl.ds(bulk, packed - bulk)]
    me_b, others_b = peers_of("basis", nb)
    me_z, others_z = state_peers(nz)
    low = lax.broadcasted_iota(jnp.int32, (lev, LANES), 1) < LANES // 2

    def to_basis(q, s, peer):
        return remote(
            outgo.at[peer, q, s],
            block.at[q, s, me_b],
            b_send.at[q, s, peer],
            b_recv.at[q, s, me_b],
            "basis",
            peer,
        )

    def from_basis(q, s, peer):
        return remote(
            outgo.at[me_b, q, s],
            block.at[q, s, peer],
            b_send.at[q, s, peer],
            b_recv.at[q, s, peer],
            "basis",
            peer,
        )

    def state_out(src, dst, send, recv, q, p, peer):
        return remote(
            src.at[q, peer, :, :, pieces[p]],
            dst.at[q, me_z, :, :, pieces[p]],
            send.at[q, p, peer],
            recv.at[q, p, me_z],
            "state",
            peer,
        )

    def state_in(src, dst, send, recv, q, p, peer):
        return remote(
            src.at[q, me_z, :, :, pieces[p]],
            dst.at[q, peer, :, :, pieces[p]],
            send.at[q, p, peer],
            recv.at[q, p, peer],
            "state",
            peer,
        )

    there = (stepped, spread, z_send, z_recv)
    again = (mixed, held, y_send, y_recv)

    def home_out(q, p, source, h):
        peer = source * half + h
        return remote(
            held.at[q, source, h, :, pieces[p]],
            home.at[q, me_b, :, pieces[p]],
            c_send.at[q, p, peer],
            c_recv.at[q, p, me_b],
            "basis",
            peer,
        )

    def home_in(q, p, peer):
        return remote(
            held.at[q, 0, 0, :, pieces[p]],
            home.at[q, peer, :, pieces[p]],
            c_send.at[q, p, peer],
            c_recv.at[q, p, peer],
            "basis",
            peer,
        )

    barrier = pltpu.get_barrier_semaphore()
    for axis, size in (("basis", nb), ("state", nz)):
        for peer in peers_of(axis, size)[1]:
            pl.semaphore_signal(
                barrier, inc=1, device_id={axis: peer}, device_id_type=pl.DeviceIdType.MESH
            )
    loads = [pltpu.make_async_copy(x_ref.at[s], xin.at[s], in_sem.at[s]) for s in range(ns)]
    for load in loads:
        load.start()
    kron_left(ms_ref[...], lev, kh, kl)
    xs[...] = jnp.zeros_like(xs)
    for s in range(ns):
        loads[s].wait()
        for i in range(m):
            xs[i * lev : (i + 1) * lev, :cols] = xin[s, :, i * cols : (i + 1) * cols]
        xh, xl = split2(xs[...])
        y = bdot(kh[...], xh) + bdot(kl[...], xh) + bdot(kh[...], xl)
        outgo[:, :, s] = y.reshape(nb, nq, lev, width)
        if s == 0:
            pl.semaphore_wait(barrier, nb + nz - 2)
        for peer in others_b:
            to_basis(0, s, peer).start()

    @pl.loop(1, nq)
    def _(q):
        for s in range(ns):
            for peer in others_b:
                to_basis(q, s, peer).start()

    kron_lanes(fk_ref[...].T, GROUP_BLOCKS, fh, fl)
    kron_lanes(bk_ref[...].T, GROUP_BLOCKS, bh, bl)
    tile_m = (
        lax.rem(lax.broadcasted_iota(jnp.int32, (m, group), 1), m)
        == lax.broadcasted_iota(jnp.int32, (m, group), 0)
    ).astype(jnp.float32)
    cps[...] = jnp.dot(cp_ref[...].T, tile_m, precision=lax.Precision.HIGHEST)
    ch, cl = split2(fc_ref[...])
    dh, dl = split2(bc_ref[...])

    @pl.loop(0, nq)
    def _(q):
        for s in range(ns):
            block[q, s, me_b] = outgo[me_b, q, s]
            for peer in others_b:
                from_basis(q, s, peer).wait_recv()
            work[...] = left3(ch, cl, block[q, s].reshape(c_all, width))
            for at in range(0, width, group):
                n = min(group, width - at)
                g = right3(work[:, at : at + n], fh[:n, :n], fl[:n, :n]) * cps[:, :n]
                work[:, at : at + n] = right3(g, bh[:n, :n], bl[:n, :n])
            y = left3(dh, dl, work[...])
            stepped[q, :, :, :, s * bulk : (s + 1) * bulk] = y[:, :bulk].reshape(
                nz, half, lev, bulk
            )
            tail = y[:, bulk:]
            if s == 0:
                first_tail = tail
            else:
                tail = jnp.where(
                    lax.broadcasted_iota(jnp.int32, tail.shape, 1) < LANES // 2,
                    first_tail,
                    pltpu.roll(tail, LANES // 2, 1),
                )
                stepped[q, :, :, :, packed - LANES :] = tail.reshape(nz, half, lev, LANES)
            for peer in others_z:
                state_out(*there, q, s, peer).start()
        spread[q, me_z] = stepped[q, me_z]

    pairs = [(a, b) for a in range(total) for b in range(a + 1)]

    def gram_chunk(q, accs):
        accs = list(accs)
        for p in range(ns):
            for peer in others_z:
                state_in(*there, q, p, peer).wait_recv()
        for h in range(half):
            for _, vals in bulk_tiles(spread, q, h, low, nz, ns):
                for p, (a, b) in enumerate(pairs):
                    accs[p] = accs[p] + vals[a] * vals[b]
        return tuple(accs)

    zero = jnp.zeros((lev, LANES), jnp.float32)
    accs = lax.fori_loop(0, nq, gram_chunk, (zero,) * len(pairs))
    row = lax.broadcasted_iota(jnp.int32, (total, LANES), 0)
    col = lax.broadcasted_iota(jnp.int32, (total, LANES), 1)
    partial = jnp.zeros((total, LANES), jnp.float32)
    for p, (a, b) in enumerate(pairs):
        v = jnp.sum(jnp.sum(accs[p], axis=0, keepdims=True), axis=1, keepdims=True)
        here = ((row == a) & (col == b)) | ((row == b) & (col == a))
        partial = jnp.where(here, v, partial)

    def share(slots, send, recv, axis, me, others, value):
        slots[me] = value
        for peer in others:
            remote(slots.at[me], slots.at[me], send.at[peer], recv.at[me], axis, peer).start()
        for peer in others:
            remote(slots.at[me], slots.at[peer], send.at[peer], recv.at[peer], axis, peer).wait()
        out = slots[0]
        for i in range(1, slots.shape[0]):
            out = out + slots[i]
        return out

    partial = share(gram_b, gb_send, gb_recv, "basis", me_b, others_b, partial)
    gram = share(gram_z, gz_send, gz_recv, "state", me_z, others_z, partial)
    gram = gram / float(c_all * m * cols)
    pair = jnp.where(col == row + total, 1.0, gram)
    diag = jnp.ones((total, 1), jnp.float32)
    for j in range(total):
        pivot = pair[j : j + 1, j : j + 1]
        diag = jnp.where(row[:, :1] == j, pivot, diag)
        if j < total - 1:
            factor = jnp.where(row[:, :1] > j, pair[:, j : j + 1] / pivot, 0.0)
            pair = pair - factor * pair[j : j + 1, :]
    pair = pair / jnp.sqrt(diag)
    for b in range(total):
        for a in range(total):
            splat[b * total + a] = jnp.broadcast_to(
                pair[b : b + 1, total + a : total + a + 1], (lev, LANES)
            )

    @pl.loop(0, nq)
    def _(q):
        for p in range(ns):
            for h in range(half):
                for t, vals in bulk_tiles(spread, q, h, low, nz, ns):
                    if t is None and p < ns - 1:
                        continue
                    for z in range(nz):
                        outs = []
                        for s in range(ns) if t is None else (p,):
                            b = z * ns + s
                            acc = splat[b * total] * vals[0]
                            for a in range(1, total):
                                acc = acc + splat[b * total + a] * vals[a]
                            outs.append(acc)
                        if t is None:
                            mixed[q, z, h, :, packed - LANES :] = jnp.where(
                                low, outs[0], pltpu.roll(outs[1], LANES // 2, 1)
                            )
                        else:
                            at = p * bulk + t * LANES
                            mixed[q, z, h, :, at : at + LANES] = outs[0]
            for peer in others_z:
                state_out(*again, q, p, peer).start()
        held[q, me_z] = mixed[q, me_z]

    def hand_on(q, p, source):
        for h in range(half):
            mine = source * half + h == me_b

            @pl.when(jnp.logical_not(mine))
            def _():
                home_out(q, p, source, h).start()

            @pl.when(mine)
            def _():
                home[q, me_b, :, pieces[p]] = held[q, source, h, :, pieces[p]]

    @pl.loop(0, nq)
    def _(q):
        for p in range(ns):
            hand_on(q, p, me_z)

    def place(q, p):
        for peer in others_b:
            home_in(q, p, peer).wait_recv()
        for b in range(nb):
            at = (b * nq + q) * cols
            o_ref[p, :, at : at + bulk] = home[q, b, :, p * bulk : (p + 1) * bulk]
            if p == ns - 1:
                for s in range(ns):
                    tail = packed - LANES + s * (cols - bulk)
                    o_ref[s, :, at + bulk : at + cols] = home[q, b, :, tail : tail + cols - bulk]

    order = [(q, p) for q in range(nq) for p in range(ns)]
    for k, (q, p) in enumerate(order):
        for peer in others_z:
            state_in(*again, q, p, peer).wait_recv()
            hand_on(q, p, peer)
        if k > 0:
            place(*order[k - 1])
    place(*order[-1])

    @pl.loop(0, nq)
    def _(q):
        for p in range(ns):
            for peer in others_b:
                to_basis(q, p, peer).wait_send()
                home_in(q, p, peer).wait_send()
            for peer in others_z:
                state_out(*there, q, p, peer).wait_send()
                state_out(*again, q, p, peer).wait_send()


def fast_body(
    nz,
    nb,
    states,
    membrane_step,
    cavity_forward,
    coupling,
    membrane_forward,
    cavity_back,
    membrane_back,
):
    f32, bf16 = jnp.float32, jnp.bfloat16
    ns, lev, joint = states.shape
    m = membrane_step.shape[0]
    c_all = cavity_forward.shape[0]
    nq, half = m // nb, nb // nz
    cols = joint // m
    width = -(-cols // LANES) * LANES
    group = m * GROUP_BLOCKS
    total = nz * ns
    dma = pltpu.SemaphoreType.DMA
    vmem = pl.BlockSpec(memory_space=pltpu.VMEM)
    panel = (nq, nz, half, lev, ns * cols)
    return pl.pallas_call(
        functools.partial(step_kernel, nz, nb),
        in_specs=[pl.BlockSpec(memory_space=pl.ANY)] + [vmem] * 6,
        out_specs=vmem,
        out_shape=jax.ShapeDtypeStruct((ns, lev, joint), f32),
        scratch_shapes=[
            pltpu.VMEM((ns, lev, joint), f32),
            pltpu.VMEM((m * lev, m * lev), bf16),
            pltpu.VMEM((m * lev, m * lev), bf16),
            pltpu.VMEM((m * lev, width), f32),
            pltpu.VMEM((nb, nq, ns, lev, width), f32),
        ]
        + [pltpu.VMEM((group, group), bf16)] * 4
        + [
            pltpu.VMEM((c_all, group), f32),
            pltpu.VMEM((c_all, width), f32),
            pltpu.VMEM((nq, ns, nb, lev, width), f32),
            pltpu.VMEM(panel, f32),
            pltpu.VMEM(panel, f32),
            pltpu.VMEM((nb, total, LANES), f32),
            pltpu.VMEM((nz, total, LANES), f32),
            pltpu.VMEM((total * total, lev, LANES), f32),
            pltpu.VMEM(panel, f32),
            pltpu.VMEM(panel, f32),
            pltpu.VMEM((nq, nb, lev, ns * cols), f32),
            dma((ns,)),
        ]
        + [dma((nq, ns, nb))] * 2
        + [dma((nq, ns, nz))] * 2
        + [dma((nb,))] * 2
        + [dma((nz,))] * 2
        + [dma((nq, ns, nz))] * 2
        + [dma((nq, ns, nb))] * 2,
        compiler_params=pltpu.CompilerParams(
            vmem_limit_bytes=VMEM_LIMIT, collective_id=0, has_side_effects=True
        ),
    )(
        states,
        membrane_step,
        cavity_forward,
        coupling.T,
        membrane_forward,
        cavity_back,
        membrane_back,
    )


def solution(mesh):
    nz, nb = mesh.shape["state"], mesh.shape["basis"]
    in_specs = (P("state", "basis", None), P(), P(), P(), P(), P(), P())
    out_specs = P("state", "basis", None)

    def body(states, membrane_step, cavity_forward, *rest):
        m, c_all = membrane_step.shape[0], cavity_forward.shape[0]
        divides = m % nb == 0 and nb % nz == 0 and nb % 2 == 0
        packs = states.shape[0] == 2 and m * m % LANES == LANES // 2
        if divides and packs and states.shape[1] == 8 and c_all == 8 * nb:
            return fast_body(nz, nb, states, membrane_step, cavity_forward, *rest)
        return plain_body(states, membrane_step, cavity_forward, *rest)

    return jax.shard_map(body, mesh=mesh, in_specs=in_specs, out_specs=out_specs, check_vma=False)
```

profile of v0, /device:TPU:25, one launch (start us, length us, event | category | flops | bytes accessed | tf_op | source)
XLA Modules:
  0.0 214.6 jit_solution(13933577174222236190)
XLA Ops:
  0.0 210.2 %shard_map.73 = f32[2,8,64000]{2,1,0:T(8,128)} custom-call(f32[2,8,64000]{2,1,0:T(8,128)} %x_ref.1, f32[40,40]{1,0:T(8,128)} %ms_ref.1, f32[64,64]{1,0:T(8,128)} %fc_ref.1, f32[40,64]{1,0:T(8,128)} %bitcast.1, f32[40,40]{1,0:T(8,128)} %fk_ref.1, f32[64,64]{1,0:T(8,128)} %bc_ref.1, f32[40,40]{1,0:T(8,128)} %bk_ref.1), custom_call_target="tpu_custom_call" | custom-call | tf_op jit(solution)/shard_map/pallas_call | solution.py:497
  210.2 4.4 %copy.9 = f32[2,8,64000]{2,1,0:T(8,128)} copy(f32[2,8,64000]{2,1,0:T(8,128)} %shard_map.73) | data formatting | bytes 8192000
where the time goes:
time: 218 us; the launch traced here: 215 us
  Pallas kernels  210 us (96%)
  local copies, waits for them, and re-layouts  4.4 us (2%)
    pallas_call x1, Pallas kernels, fast_body(): pl.pallas_call(functools.partial(step_kernel, nz, nb), in_specs=[pl.Block...  210 us
    unnamed x1, local copies, waits for them, and re-layouts  4.4 us

commit v1 on v0

v1 whole, which is shorter than its diff:
```python
import functools

import jax
import jax.numpy as jnp
from jax import lax
from jax.experimental import pallas as pl
from jax.experimental.pallas import tpu as pltpu
from jax.sharding import PartitionSpec as P

LANES = 128
GROUP_BLOCKS = 16
VMEM_LIMIT = 60 * 1024 * 1024
DIRECT = 2
AHEAD = 1
LAG = 1


def plain_body(
    states, membrane_step, cavity_forward, coupling, membrane_forward, cavity_back, membrane_back
):
    highest = lax.Precision.HIGHEST
    panel_size, level_count, joint = states.shape
    levels_all = cavity_forward.shape[0]
    membrane_levels = membrane_step.shape[0]
    basis_total = float(levels_all * joint)
    head = jnp.einsum(
        "ab,scbr->scar",
        membrane_step,
        states.reshape(panel_size, level_count, membrane_levels, joint // membrane_levels),
        precision=highest,
    )
    head = head.reshape(panel_size, level_count, joint)
    panel_block = lax.all_to_all(head, "basis", split_axis=2, concat_axis=1, tiled=True)
    items, cavity_all, columns = panel_block.shape
    grid = jnp.einsum("qc,kcr->kqr", cavity_forward, panel_block, precision=highest)
    grid = jnp.einsum(
        "kqtm,nm->kqtn",
        grid.reshape(items, cavity_all, columns // membrane_levels, membrane_levels),
        membrane_forward,
        precision=highest,
    )
    weighted = grid * coupling[None, :, None, :]
    backward = jnp.einsum("kqtn,mn->kqtm", weighted, membrane_back, precision=highest)
    backward = backward.reshape(items, cavity_all, columns)
    stepped = jnp.einsum("cq,kqr->kcr", cavity_back, backward, precision=highest)
    spread = lax.all_to_all(stepped, "state", split_axis=2, concat_axis=0, tiled=True)
    state_total, spread_levels, spread_cols = spread.shape
    flattened = spread.reshape(state_total, -1)
    partial_gram = jnp.dot(flattened, flattened.T, precision=highest)
    gram = lax.psum(partial_gram, ("state", "basis")) / basis_total
    lower_factor = jnp.linalg.cholesky(gram)
    identity = jnp.eye(state_total, dtype=gram.dtype)
    inverse = lax.linalg.triangular_solve(lower_factor, identity, left_side=True, lower=True)
    local_result = jnp.dot(inverse, flattened, precision=highest)
    local_result = local_result.reshape(state_total, spread_levels, spread_cols)
    return lax.all_to_all(
        lax.all_to_all(local_result, "state", split_axis=0, concat_axis=2, tiled=True),
        "basis",
        split_axis=1,
        concat_axis=2,
        tiled=True,
    )


def split2(x):
    hi = x.astype(jnp.bfloat16)
    lo = (x - hi.astype(jnp.float32)).astype(jnp.bfloat16)
    return hi, lo


def bdot(a, b):
    return jnp.dot(a, b, preferred_element_type=jnp.float32)


def left3(wh, wl, x):
    xh, xl = split2(x)
    return bdot(jnp.concatenate([wh, wl, wh], axis=1), jnp.concatenate([xh, xh, xl], axis=0))


def right3(x, wh, wl):
    xh, xl = split2(x)
    return bdot(xh, wh) + bdot(xl, wh) + bdot(xh, wl)


def kron_left(w, reps, out_ref_h, out_ref_l):
    m = w.shape[0]
    n = m * reps
    row = lax.broadcasted_iota(jnp.int32, (n, m), 0)
    col = lax.broadcasted_iota(jnp.int32, (n, m), 1)
    left = (row // reps == col).astype(jnp.bfloat16)
    right_row = lax.broadcasted_iota(jnp.int32, (m, n), 0)
    right_col = lax.broadcasted_iota(jnp.int32, (m, n), 1)
    right = (right_col // reps == right_row).astype(jnp.bfloat16)
    a = lax.broadcasted_iota(jnp.int32, (n, 1), 0)
    b = lax.broadcasted_iota(jnp.int32, (1, n), 1)
    keep = lax.rem(a, reps) == lax.rem(b, reps)
    for part, ref in zip(split2(w), (out_ref_h, out_ref_l)):
        full = bdot(bdot(left, part).astype(jnp.bfloat16), right)
        ref[...] = jnp.where(keep, full, 0.0).astype(jnp.bfloat16)


def kron_lanes(w_t, reps, out_ref_h, out_ref_l):
    m = w_t.shape[0]
    n = m * reps
    left = (
        lax.rem(lax.broadcasted_iota(jnp.int32, (n, m), 0), m)
        == lax.broadcasted_iota(jnp.int32, (n, m), 1)
    ).astype(jnp.bfloat16)
    right = (
        lax.rem(lax.broadcasted_iota(jnp.int32, (m, n), 1), m)
        == lax.broadcasted_iota(jnp.int32, (m, n), 0)
    ).astype(jnp.bfloat16)
    a = lax.broadcasted_iota(jnp.int32, (n, 1), 0)
    b = lax.broadcasted_iota(jnp.int32, (1, n), 1)
    keep = a // m == b // m
    for part, ref in zip(split2(w_t), (out_ref_h, out_ref_l)):
        full = bdot(bdot(left, part).astype(jnp.bfloat16), right)
        ref[...] = jnp.where(keep, full, 0.0).astype(jnp.bfloat16)


def remote(src, dst, send_sem, recv_sem, axis, peer):
    return pltpu.make_async_remote_copy(
        src_ref=src,
        dst_ref=dst,
        send_sem=send_sem,
        recv_sem=recv_sem,
        device_id={axis: peer},
        device_id_type=pl.DeviceIdType.MESH,
    )


def peers_of(axis, size):
    me = lax.axis_index(axis)
    return me, [lax.rem(me + d, size) for d in range(1, size)]


def lane_groups(cols, group):
    out = []
    for at in range(0, cols, group):
        n = min(group, cols - at)
        out.append((at, n, -(-n // LANES) * LANES))
    return out


def tiles_of(at, n, ns):
    for t in range(n // LANES):
        yield [ns * at + s * (n // LANES) * LANES + t * LANES for s in range(ns)]
    if n % LANES:
        yield [ns * at + ns * (n // LANES) * LANES]


def load_pair(ref, low, offs):
    vals = [ref[:, at : at + LANES] for at in offs]
    if len(vals) == 1:
        v = vals[0]
        vals = [jnp.where(low, v, 0.0), jnp.where(low, pltpu.roll(v, LANES // 2, 1), 0.0)]
    return vals


def store_pair(ref, low, offs, vals):
    if len(offs) == 1:
        vals = [jnp.where(low, vals[0], pltpu.roll(vals[1], LANES // 2, 1))]
    for at, v in zip(offs, vals):
        ref[:, at : at + LANES] = v


def step_kernel(
    nz,
    nb,
    x_ref,
    ms_ref,
    fc_ref,
    cp_ref,
    fk_ref,
    bc_ref,
    bk_ref,
    o_ref,
    xin,
    kh,
    kl,
    xs,
    outgo,
    fh,
    fl,
    bh,
    bl,
    cps,
    block,
    panels,
    gacc,
    gram_b,
    gram_z,
    splat,
    mixed,
    sums,
    home,
    in_sem,
    b_send,
    b_recv,
    z_send,
    z_recv,
    gb_send,
    gb_recv,
    gz_send,
    gz_recv,
    c_send,
    c_recv,
):
    ns, lev, _ = xin.shape
    nq = block.shape[0]
    rows = nb // 2
    total = nz * ns
    c_all = fc_ref.shape[0]
    m = fk_ref.shape[0]
    cols = x_ref.shape[2] // m
    group = m * GROUP_BLOCKS
    groups = lane_groups(cols, group)
    ng = len(groups)
    padded = [pl.ds(ns * at, ns * wide) for at, _, wide in groups]
    packed = [pl.ds(ns * at, ns * n) for at, n, _ in groups]
    me_b, others_b = peers_of("basis", nb)
    me_z, others_z = peers_of("state", nz)
    parity = lax.rem(me_b, 2)
    inner = (me_z == 1) | (me_z == 2)
    low = lax.broadcasted_iota(jnp.int32, (lev, LANES), 1) < LANES // 2

    def to_basis(q, g, peer):
        return remote(
            outgo.at[peer, q, :, padded[g]],
            block.at[q, me_b, :, padded[g]],
            b_send.at[q, g, peer],
            b_recv.at[q, g, me_b],
            "basis",
            peer,
        )

    def from_basis(q, g, peer):
        return remote(
            outgo.at[me_b, q, :, padded[g]],
            block.at[q, peer, :, padded[g]],
            b_send.at[q, g, peer],
            b_recv.at[q, g, peer],
            "basis",
            peer,
        )

    def along(src, slot, q, h, g, peer):
        return remote(
            src.at[q, h, :, :, packed[g]],
            panels.at[slot, q, h, :, :, packed[g]],
            z_send.at[slot, q, h, g],
            z_recv.at[slot, q, h, g],
            "state",
            peer,
        )

    def push(k, q, h, g, peer):
        along(panels.at[k], k, q, h, g, peer).start()

    def arrived(slot, q, h, g):
        along(mixed, slot, q, h, g, others_z[0]).wait_recv()

    def sent(slot, q, h, g):
        along(mixed, slot, q, h, g, others_z[0]).wait_send()

    def home_out(q, h, g, r):
        peer = 2 * r + h
        return remote(
            mixed.at[q, h, r, :, packed[g]],
            home.at[q, me_b, :, packed[g]],
            c_send.at[q, g, peer],
            c_recv.at[q, g, me_b],
            "basis",
            peer,
        )

    def home_in(q, g, peer):
        return remote(
            mixed.at[q, 0, 0, :, packed[g]],
            home.at[q, peer, :, packed[g]],
            c_send.at[q, g, peer],
            c_recv.at[q, g, peer],
            "basis",
            peer,
        )

    barrier = pltpu.get_barrier_semaphore()
    for axis, others in (("basis", others_b), ("state", others_z)):
        for peer in others:
            pl.semaphore_signal(
                barrier, inc=1, device_id={axis: peer}, device_id_type=pl.DeviceIdType.MESH
            )
    loads = [pltpu.make_async_copy(x_ref.at[s], xin.at[s], in_sem.at[s]) for s in range(ns)]
    for load in loads:
        load.start()
    kron_left(ms_ref[...], lev, kh, kl)
    gacc[...] = jnp.zeros_like(gacc)
    for load in loads:
        load.wait()
    for g, (at, n, wide) in enumerate(groups):
        for i in range(m):
            for s in range(ns):
                xs[i * lev : (i + 1) * lev, s * wide : s * wide + n] = xin[
                    s, :, i * cols + at : i * cols + at + n
                ]
        xh, xl = split2(xs[:, : ns * wide])
        y = bdot(kh[...], xh) + bdot(kl[...], xh) + bdot(kh[...], xl)
        outgo[:, :, :, padded[g]] = y.reshape(nb, nq, lev, ns * wide)
        if g == 0:
            pl.semaphore_wait(barrier, nb + nz - 2)
        for peer in others_b:
            to_basis(0, g, peer).start()
        if g == 0:
            kron_lanes(fk_ref[...].T, GROUP_BLOCKS, fh, fl)
            kron_lanes(bk_ref[...].T, GROUP_BLOCKS, bh, bl)
            tile_m = (
                lax.rem(lax.broadcasted_iota(jnp.int32, (m, group), 1), m)
                == lax.broadcasted_iota(jnp.int32, (m, group), 0)
            ).astype(jnp.float32)
            factor = jnp.dot(cp_ref[...].T, tile_m, precision=lax.Precision.HIGHEST)
            for s in range(ns):
                cps[s * c_all : (s + 1) * c_all] = factor

    @pl.loop(1, nq)
    def _(q):
        for g in range(ng):
            for peer in others_b:
                to_basis(q, g, peer).start()

    ch, cl = split2(fc_ref[...])
    dh, dl = split2(bc_ref[...])
    far, relay_half, gram_half = 3 * (me_z - 1), me_z - 1, 2 - me_z

    def relay(q):
        for g in range(ng):
            arrived(far, q, relay_half, g)
            push(far, q, relay_half, g, 3 - me_z)

    @pl.loop(0, nq)
    def _(q):
        for g, (at, n, wide) in enumerate(groups):
            block[q, me_b, :, padded[g]] = outgo[me_b, q, :, padded[g]]
            for peer in others_b:
                from_basis(q, g, peer).wait_recv()
            y = left3(ch, cl, block[q, :, :, padded[g]].reshape(c_all, ns * wide))
            y = jnp.concatenate([y[:, s * wide : (s + 1) * wide] for s in range(ns)], axis=0)
            y = right3(y, fh[:wide, :wide], fl[:wide, :wide]) * cps[:, :wide]
            y = right3(y, bh[:wide, :wide], bl[:wide, :wide])
            y = jnp.concatenate([y[s * c_all : (s + 1) * c_all] for s in range(ns)], axis=1)
            y = left3(dh, dl, y)
            if n % LANES:
                full = n - n % LANES
                edge = [y[:, s * wide + full : s * wide + full + LANES] for s in range(ns)]
                wide_low = lax.broadcasted_iota(jnp.int32, edge[0].shape, 1) < LANES // 2
                edge = jnp.where(wide_low, edge[0], pltpu.roll(edge[1], LANES // 2, 1))
                y = jnp.concatenate(
                    [y[:, s * wide : s * wide + full] for s in range(ns)] + [edge], axis=1
                )
            y = y.reshape(rows, 2, lev, ns * n)
            for h in range(2):
                panels[me_z, q, h, :, :, packed[g]] = y[:, h]

            @pl.when(me_z == 0)
            def _():
                push(0, q, 0, g, 1)
                push(0, q, 1, g, 1)

            @pl.when(me_z == 1)
            def _():
                push(1, q, 0, g, 2)

            @pl.when(me_z == 2)
            def _():
                push(2, q, 1, g, 1)

                @pl.when(q < DIRECT)
                def _():
                    push(2, q, 0, g, 3)

            @pl.when(me_z == 3)
            def _():
                push(3, q, 1, g, 2)
                push(3, q, 0, g, 2)

        @pl.when(inner & (q >= 1) & (q <= 2))
        def _():
            relay(q - 1)

    pairs = [(a, b) for a in range(total) for b in range(a + 1)]

    def second(q, g):
        push(1, q, 1, g, 2)
        push(0, q, 1, g, 2)

    def gram_piece(q, h):
        def body(r, accs):
            accs = list(accs)
            for at, n, _ in groups:
                for offs in tiles_of(at, n, ns):
                    vals = []
                    for k in range(nz):
                        vals += load_pair(panels.at[k, q, h, r], low, offs)
                    for p, (a, b) in enumerate(pairs):
                        accs[p] = accs[p] + vals[a] * vals[b]
            return tuple(accs)

        zero = jnp.zeros((lev, LANES), jnp.float32)
        for p, acc in enumerate(lax.fori_loop(0, rows, body, (zero,) * len(pairs))):
            gacc[p] += acc

    row = lax.broadcasted_iota(jnp.int32, (total, LANES), 0)
    col = lax.broadcasted_iota(jnp.int32, (total, LANES), 1)

    @pl.when(inner)
    def _():
        relay(2)

        @pl.loop(0, nq)
        def _(q):
            @pl.when(q == 2)
            def _():
                relay(3)

            @pl.when(q == 3)
            def _():
                relay(4)

                @pl.when(me_z == 1)
                def _():
                    for g in range(AHEAD):
                        second(0, g)

            for g in range(ng):
                arrived(0, q, gram_half, g)
                arrived(3, q, gram_half, g)
                arrived(3 - me_z, q, gram_half, g)

            @pl.when((me_z == 2) & (q < DIRECT))
            def _():
                for g in range(ng):
                    push(1, q, 0, g, 3)
                    push(0, q, 0, g, 3)

            gram_piece(q, gram_half)

        partial = jnp.zeros((total, LANES), jnp.float32)
        for p, (a, b) in enumerate(pairs):
            v = jnp.sum(jnp.sum(gacc[p], axis=0, keepdims=True), axis=1, keepdims=True)
            here = ((row == a) & (col == b)) | ((row == b) & (col == a))
            partial = jnp.where(here, v, partial)
        gram_b[me_b] = partial
        for peer in others_b:
            remote(
                gram_b.at[me_b],
                gram_b.at[me_b],
                gb_send.at[peer],
                gb_recv.at[me_b],
                "basis",
                peer,
            ).start()
        for peer in others_b:
            remote(
                gram_b.at[me_b],
                gram_b.at[peer],
                gb_send.at[peer],
                gb_recv.at[peer],
                "basis",
                peer,
            ).wait()
        partial = gram_b[0]
        for i in range(1, nb):
            partial = partial + gram_b[i]
        gram_z[me_z] = partial
        for peer in others_z:
            remote(
                gram_z.at[me_z],
                gram_z.at[me_z],
                gz_send.at[peer],
                gz_recv.at[me_z],
                "state",
                peer,
            ).start()

        @pl.when(me_z == 1)
        def _():
            for g in range(AHEAD, ng):
                second(0, g)

            @pl.loop(1, nq)
            def _(q):
                for g in range(ng):
                    second(q, g)

    for source in (1, 2):
        @pl.when(me_z != source)
        def _():
            remote(
                gram_z.at[source],
                gram_z.at[source],
                gz_send.at[source],
                gz_recv.at[source],
                "state",
                others_z[0],
            ).wait_recv()

    gram = (gram_z[1] + gram_z[2]) / float(c_all * m * cols)
    pair = jnp.where(col == row + total, 1.0, gram)
    diag = jnp.ones((total, 1), jnp.float32)
    for j in range(total):
        pivot = pair[j : j + 1, j : j + 1]
        diag = jnp.where(row[:, :1] == j, pivot, diag)
        if j < total - 1:
            factor = jnp.where(row[:, :1] > j, pair[:, j : j + 1] / pivot, 0.0)
            pair = pair - factor * pair[j : j + 1, :]
    pair = pair / jnp.sqrt(diag)
    for b in range(total):
        for a in range(b + 1):
            splat[b * total + a] = jnp.broadcast_to(
                pair[b : b + 1, total + a : total + a + 1], (lev, LANES)
            )

    def mix(q, h, g, ins, outs):
        at, n, _ = groups[g]

        @pl.loop(0, rows)
        def _(r):
            for offs in tiles_of(at, n, ns):
                vals = {k: load_pair(panels.at[k, q, h, r], low, offs) for k, _ in ins}
                for panel, dst in outs:
                    res = []
                    for s in range(ns):
                        b = panel * ns + s
                        acc = None
                        for k, ready in ins:
                            if ready:
                                terms = [vals[k][s]]
                            else:
                                terms = [
                                    splat[b * total + k * ns + a] * vals[k][a]
                                    for a in range(ns)
                                    if k * ns + a <= b
                                ]
                            for term in terms:
                                acc = term if acc is None else acc + term
                        res.append(acc)
                    store_pair(dst.at[q, h, r], low, offs, res)

    def plain(*ks):
        return [(k, False) for k in ks]

    def send_home(q, h, g):
        for r in range(rows):
            mine = 2 * r + h == me_b

            @pl.when(jnp.logical_not(mine))
            def _():
                home_out(q, h, g, r).start()

            @pl.when(mine)
            def _():
                home[q, me_b, :, packed[g]] = mixed[q, h, r, :, packed[g]]

    @pl.loop(0, nq)
    def _(q):
        for g in range(ng):
            @pl.when(me_z == 0)
            def _():
                for h in range(2):
                    mix(q, h, g, plain(0), [(0, mixed)])

            @pl.when(me_z == 1)
            def _():
                for h in range(2):
                    mix(q, h, g, plain(0, 1), [(1, mixed)])

            @pl.when(me_z == 2)
            def _():
                mix(q, 0, g, plain(0, 1, 2), [(2, mixed), (3, sums)])

                @pl.when(q >= DIRECT)
                def _():
                    along(sums, 0, q, 0, g, 3).start()

            @pl.when(me_z == 3)
            def _():
                arrived(0, q, 0, g)

                @pl.when(q < DIRECT)
                def _():
                    arrived(1, q, 0, g)
                    arrived(2, q, 0, g)
                    mix(q, 0, g, plain(0, 1, 2, 3), [(3, mixed)])

                @pl.when(q >= DIRECT)
                def _():
                    mix(q, 0, g, [(0, True), (3, False)], [(3, mixed)])

            send_home(q, 0, g)

            @pl.when(me_z <= 1)
            def _():
                send_home(q, 1, g)

    def place(q, g):
        at, n, _ = groups[g]
        full = n - n % LANES
        for peer in others_b:
            home_in(q, g, peer).wait_recv()
        for b in range(nb):
            lane = (b * nq + q) * cols + at
            for s in range(ns):
                src = ns * at + s * full
                o_ref[s, :, lane : lane + full] = home[q, b, :, src : src + full]
                if n % LANES:
                    src = ns * at + ns * full + s * (n - full)
                    o_ref[s, :, lane + full : lane + n] = home[q, b, :, src : src + n - full]

    order = [(q, g) for q in range(nq) for g in range(ng)]
    for k, (q, g) in enumerate(order):
        @pl.when(me_z == 2)
        def _():
            arrived(0, q, 1, g)
            arrived(1, q, 1, g)
            mix(q, 1, g, plain(0, 1, 2), [(2, mixed), (3, sums)])
            along(sums, 0, q, 1, g, 3).start()

        @pl.when(me_z == 3)
        def _():
            arrived(0, q, 1, g)
            mix(q, 1, g, [(0, True), (3, False)], [(3, mixed)])

        @pl.when(me_z >= 2)
        def _():
            send_home(q, 1, g)

        if k >= LAG:
            place(*order[k - LAG])
    for k in range(len(order) - LAG, len(order)):
        place(*order[k])

    @pl.loop(0, nq)
    def _(q):
        for g in range(ng):
            for peer in others_b:
                to_basis(q, g, peer).wait_send()
                home_in(q, g, peer).wait_send()

            @pl.when(me_z == 0)
            def _():
                for h in range(2):
                    sent(0, q, h, g)

            @pl.when(me_z == 1)
            def _():
                for k in range(2):
                    for h in range(2):
                        sent(k, q, h, g)

            @pl.when(me_z == 2)
            def _():
                sent(2, q, 1, g)
                sent(3, q, 1, g)
                sent(0, q, 0, g)
                sent(0, q, 1, g)

                @pl.when(q < DIRECT)
                def _():
                    sent(1, q, 0, g)
                    sent(2, q, 0, g)

            @pl.when(me_z == 3)
            def _():
                for h in range(2):
                    sent(3, q, h, g)

    @pl.when(inner)
    def _():
        for peer in others_z:
            remote(
                gram_z.at[me_z],
                gram_z.at[me_z],
                gz_send.at[peer],
                gz_recv.at[me_z],
                "state",
                peer,
            ).wait_send()


def fast_body(
    nz,
    nb,
    states,
    membrane_step,
    cavity_forward,
    coupling,
    membrane_forward,
    cavity_back,
    membrane_back,
):
    f32, bf16 = jnp.float32, jnp.bfloat16
    ns, lev, joint = states.shape
    m = membrane_step.shape[0]
    c_all = cavity_forward.shape[0]
    nq, rows = m // nb, nb // 2
    cols = joint // m
    group = m * GROUP_BLOCKS
    groups = lane_groups(cols, group)
    ng = len(groups)
    width = sum(wide for _, _, wide in groups)
    total = nz * ns
    dma = pltpu.SemaphoreType.DMA
    vmem = pl.BlockSpec(memory_space=pltpu.VMEM)
    panel = (nq, 2, rows, lev, ns * cols)
    return pl.pallas_call(
        functools.partial(step_kernel, nz, nb),
        in_specs=[pl.BlockSpec(memory_space=pl.ANY)] + [vmem] * 6,
        out_specs=vmem,
        out_shape=jax.ShapeDtypeStruct((ns, lev, joint), f32),
        scratch_shapes=[
            pltpu.VMEM((ns, lev, joint), f32),
            pltpu.VMEM((m * lev, m * lev), bf16),
            pltpu.VMEM((m * lev, m * lev), bf16),
            pltpu.VMEM((m * lev, ns * group), f32),
            pltpu.VMEM((nb, nq, lev, ns * width), f32),
        ]
        + [pltpu.VMEM((group, group), bf16)] * 4
        + [
            pltpu.VMEM((ns * c_all, group), f32),
            pltpu.VMEM((nq, nb, lev, ns * width), f32),
            pltpu.VMEM((nz,) + panel, f32),
            pltpu.VMEM((total * (total + 1) // 2, lev, LANES), f32),
            pltpu.VMEM((nb, total, LANES), f32),
            pltpu.VMEM((nz, total, LANES), f32),
            pltpu.VMEM((total * total, lev, LANES), f32),
            pltpu.VMEM(panel, f32),
            pltpu.VMEM(panel, f32),
            pltpu.VMEM((nq, nb, lev, ns * cols), f32),
            dma((ns,)),
        ]
        + [dma((nq, ng, nb))] * 2
        + [dma((nz, nq, 2, ng))] * 2
        + [dma((nb,))] * 2
        + [dma((nz,))] * 2
        + [dma((nq, ng, nb))] * 2,
        compiler_params=pltpu.CompilerParams(
            vmem_limit_bytes=VMEM_LIMIT, collective_id=0, has_side_effects=True
        ),
    )(
        states,
        membrane_step,
        cavity_forward,
        coupling.T,
        membrane_forward,
        cavity_back,
        membrane_back,
    )


def solution(mesh):
    nz, nb = mesh.shape["state"], mesh.shape["basis"]
    in_specs = (P("state", "basis", None), P(), P(), P(), P(), P(), P())
    out_specs = P("state", "basis", None)

    def body(states, membrane_step, cavity_forward, *rest):
        m, c_all = membrane_step.shape[0], cavity_forward.shape[0]
        divides = nz == 4 and m == 5 * nb and nb % 2 == 0
        packs = states.shape[0] == 2 and m * m % LANES == LANES // 2
        if divides and packs and states.shape[1] == 8 and c_all == 8 * nb:
            return fast_body(nz, nb, states, membrane_step, cavity_forward, *rest)
        return plain_body(states, membrane_step, cavity_forward, *rest)

    return jax.shard_map(body, mesh=mesh, in_specs=in_specs, out_specs=out_specs, check_vma=False)
```

time: 218 us -> 213 us (0.977); the launches traced: 215 us -> 213 us
  no operation moved by 1% of the time
where the time goes in v1:
time: 213 us
  Pallas kernels  208 us (98%)
  local copies, waits for them, and re-layouts  4.4 us (2%)
    pallas_call x1, Pallas kernels, fast_body(): pl.pallas_call(functools.partial(step_kernel, nz, nb), in_specs=[pl.Block...  208 us
    unnamed x1, local copies, waits for them, and re-layouts  4.4 us

profile of v1, /device:TPU:25, one launch (start us, length us, event | category | flops | bytes accessed | tf_op | source)
XLA Modules:
  0.0 212.7 jit_solution(5256428547741727971)
XLA Ops:
  0.0 208.3 %shard_map.73 = f32[2,8,64000]{2,1,0:T(8,128)} custom-call(f32[2,8,64000]{2,1,0:T(8,128)} %x_ref.1, f32[40,40]{1,0:T(8,128)} %ms_ref.1, f32[64,64]{1,0:T(8,128)} %fc_ref.1, f32[40,64]{1,0:T(8,128)} %bitcast.1, f32[40,40]{1,0:T(8,128)} %fk_ref.1, f32[64,64]{1,0:T(8,128)} %bc_ref.1, f32[40,40]{1,0:T(8,128)} %bk_ref.1), custom_call_target="tpu_custom_call" | custom-call | tf_op jit(solution)/shard_map/pallas_call | solution.py:714
  208.3 4.4 %copy.9 = f32[2,8,64000]{2,1,0:T(8,128)} copy(f32[2,8,64000]{2,1,0:T(8,128)} %shard_map.73) | data formatting | bytes 8192000

commit v2 on v1

--- a/solution.py
+++ b/solution.py
@@ -11,7 +11,7 @@
 GROUP_BLOCKS = 16
 VMEM_LIMIT = 60 * 1024 * 1024
 DIRECT = 2
-AHEAD = 1
+AHEAD = 3
 LAG = 1
 
 
@@ -178,6 +178,7 @@
     xin,
     kh,
     kl,
+    kcat,
     xs,
     outgo,
     fh,
@@ -290,21 +291,25 @@
             pl.semaphore_signal(
                 barrier, inc=1, device_id={axis: peer}, device_id_type=pl.DeviceIdType.MESH
             )
-    loads = [pltpu.make_async_copy(x_ref.at[s], xin.at[s], in_sem.at[s]) for s in range(ns)]
-    for load in loads:
-        load.start()
+    def load(s, c):
+        lanes = pl.ds(c * nb * cols, nb * cols)
+        return pltpu.make_async_copy(x_ref.at[s, :, lanes], xin.at[s, :, lanes], in_sem.at[s, c])
+
+    for c in range(m // nb):
+        for s in range(ns):
+            load(s, c).start()
     kron_left(ms_ref[...], lev, kh, kl)
-    gacc[...] = jnp.zeros_like(gacc)
-    for load in loads:
-        load.wait()
+    kcat[...] = jnp.concatenate([kh[...], kl[...], kh[...]], axis=1)
     for g, (at, n, wide) in enumerate(groups):
         for i in range(m):
             for s in range(ns):
+                if g == 0 and i % nb == 0:
+                    load(s, i // nb).wait()
                 xs[i * lev : (i + 1) * lev, s * wide : s * wide + n] = xin[
                     s, :, i * cols + at : i * cols + at + n
                 ]
         xh, xl = split2(xs[:, : ns * wide])
-        y = bdot(kh[...], xh) + bdot(kl[...], xh) + bdot(kh[...], xl)
+        y = bdot(kcat[...], jnp.concatenate([xh, xh, xl], axis=0))
         outgo[:, :, :, padded[g]] = y.reshape(nb, nq, lev, ns * wide)
         if g == 0:
             pl.semaphore_wait(barrier, nb + nz - 2)
@@ -327,14 +332,19 @@
             for peer in others_b:
                 to_basis(q, g, peer).start()
 
+    gacc[...] = jnp.zeros_like(gacc)
+
     ch, cl = split2(fc_ref[...])
     dh, dl = split2(bc_ref[...])
     far, relay_half, gram_half = 3 * (me_z - 1), me_z - 1, 2 - me_z
 
+    def relay_group(q, g):
+        arrived(far, q, relay_half, g)
+        push(far, q, relay_half, g, 3 - me_z)
+
     def relay(q):
         for g in range(ng):
-            arrived(far, q, relay_half, g)
-            push(far, q, relay_half, g, 3 - me_z)
+            relay_group(q, g)
 
     @pl.loop(0, nq)
     def _(q):
@@ -363,7 +373,10 @@
             @pl.when(me_z == 0)
             def _():
                 push(0, q, 0, g, 1)
-                push(0, q, 1, g, 1)
+
+                @pl.when(q > 0)
+                def _():
+                    push(0, q - 1, 1, g, 1)
 
             @pl.when(me_z == 1)
             def _():
@@ -380,11 +393,25 @@
             @pl.when(me_z == 3)
             def _():
                 push(3, q, 1, g, 2)
-                push(3, q, 0, g, 2)
-
-        @pl.when(inner & (q >= 1) & (q <= 2))
+
+                @pl.when(q > 0)
+                def _():
+                    push(3, q - 1, 0, g, 2)
+
+            past, back = (1, g + 1) if g < ng - 1 else (0, 0)
+
+            @pl.when(inner & (q >= past) & (q <= past + 1))
+            def _():
+                relay_group(q - past, back)
+
+    for g in range(ng):
+        @pl.when(me_z == 0)
         def _():
-            relay(q - 1)
+            push(0, nq - 1, 1, g, 1)
+
+        @pl.when(me_z == 3)
+        def _():
+            push(3, nq - 1, 0, g, 2)
 
     pairs = [(a, b) for a in range(total) for b in range(a + 1)]
 
@@ -720,6 +747,7 @@
             pltpu.VMEM((ns, lev, joint), f32),
             pltpu.VMEM((m * lev, m * lev), bf16),
             pltpu.VMEM((m * lev, m * lev), bf16),
+            pltpu.VMEM((m * lev, 3 * m * lev), bf16),
             pltpu.VMEM((m * lev, ns * group), f32),
             pltpu.VMEM((nb, nq, lev, ns * width), f32),
         ]
@@ -735,7 +763,7 @@
             pltpu.VMEM(panel, f32),
             pltpu.VMEM(panel, f32),
             pltpu.VMEM((nq, nb, lev, ns * cols), f32),
-            dma((ns,)),
+            dma((ns, nq)),
         ]
         + [dma((nq, ng, nb))] * 2
         + [dma((nz, nq, 2, ng))] * 2

time: 213 us -> 212 us (level)
  no operation moved by 1% of the time
where the time goes in v2:
time: 212 us; the launch traced here: 211 us
  Pallas kernels  207 us (98%)
  local copies, waits for them, and re-layouts  4.4 us (2%)
    pallas_call x1, Pallas kernels, fast_body(): pl.pallas_call(functools.partial(step_kernel, nz, nb), in_specs=[pl.Block...  207 us
    unnamed x1, local copies, waits for them, and re-layouts  4.4 us

profile of v2, /device:TPU:25, one launch (start us, length us, event | category | flops | bytes accessed | tf_op | source)
XLA Modules:
  0.0 211.3 jit_solution(17636236983706036008)
XLA Ops:
  0.0 206.9 %shard_map.73 = f32[2,8,64000]{2,1,0:T(8,128)} custom-call(f32[2,8,64000]{2,1,0:T(8,128)} %x_ref.1, f32[40,40]{1,0:T(8,128)} %ms_ref.1, f32[64,64]{1,0:T(8,128)} %fc_ref.1, f32[40,64]{1,0:T(8,128)} %bitcast.1, f32[40,40]{1,0:T(8,128)} %fk_ref.1, f32[64,64]{1,0:T(8,128)} %bc_ref.1, f32[40,40]{1,0:T(8,128)} %bk_ref.1), custom_call_target="tpu_custom_call" | custom-call | tf_op jit(solution)/shard_map/pallas_call | solution.py:741
  206.9 4.4 %copy.9 = f32[2,8,64000]{2,1,0:T(8,128)} copy(f32[2,8,64000]{2,1,0:T(8,128)} %shard_map.73) | data formatting | bytes 8192000

commit v3 on v2

--- a/solution.py
+++ b/solution.py
@@ -12,7 +12,7 @@
 VMEM_LIMIT = 60 * 1024 * 1024
 DIRECT = 2
 AHEAD = 3
-LAG = 1
+PLACED = 2
 
 
 def plain_body(
@@ -174,7 +174,7 @@
     fk_ref,
     bc_ref,
     bk_ref,
-    o_ref,
+    home,
     xin,
     kh,
     kl,
@@ -194,7 +194,6 @@
     splat,
     mixed,
     sums,
-    home,
     in_sem,
     b_send,
     b_recv,
@@ -273,6 +272,13 @@
             c_recv.at[q, g, me_b],
             "basis",
             peer,
+        )
+
+    def keep(q, h, g, r):
+        return pltpu.make_async_copy(
+            mixed.at[q, h, r, :, packed[g]],
+            home.at[q, me_b, :, packed[g]],
+            c_send.at[q, g, me_b],
         )
 
     def home_in(q, g, peer):
@@ -585,7 +591,7 @@
 
             @pl.when(mine)
             def _():
-                home[q, me_b, :, packed[g]] = mixed[q, h, r, :, packed[g]]
+                keep(q, h, g, r).start()
 
     @pl.loop(0, nq)
     def _(q):
@@ -628,49 +634,32 @@
             def _():
                 send_home(q, 1, g)
 
-    def place(q, g):
-        at, n, _ = groups[g]
-        full = n - n % LANES
-        for peer in others_b:
-            home_in(q, g, peer).wait_recv()
-        for b in range(nb):
-            lane = (b * nq + q) * cols + at
-            for s in range(ns):
-                src = ns * at + s * full
-                o_ref[s, :, lane : lane + full] = home[q, b, :, src : src + full]
-                if n % LANES:
-                    src = ns * at + ns * full + s * (n - full)
-                    o_ref[s, :, lane + full : lane + n] = home[q, b, :, src : src + n - full]
-
-    order = [(q, g) for q in range(nq) for g in range(ng)]
-    for k, (q, g) in enumerate(order):
-        @pl.when(me_z == 2)
-        def _():
-            arrived(0, q, 1, g)
-            arrived(1, q, 1, g)
-            mix(q, 1, g, plain(0, 1, 2), [(2, mixed), (3, sums)])
-            along(sums, 0, q, 1, g, 3).start()
-
-        @pl.when(me_z == 3)
-        def _():
-            arrived(0, q, 1, g)
-            mix(q, 1, g, [(0, True), (3, False)], [(3, mixed)])
-
-        @pl.when(me_z >= 2)
-        def _():
-            send_home(q, 1, g)
-
-        if k >= LAG:
-            place(*order[k - LAG])
-    for k in range(len(order) - LAG, len(order)):
-        place(*order[k])
+    @pl.loop(0, nq)
+    def _(q):
+        for g in range(ng):
+            @pl.when(me_z == 2)
+            def _():
+                arrived(0, q, 1, g)
+                arrived(1, q, 1, g)
+                mix(q, 1, g, plain(0, 1, 2), [(2, mixed), (3, sums)])
+                along(sums, 0, q, 1, g, 3).start()
+
+            @pl.when(me_z == 3)
+            def _():
+                arrived(0, q, 1, g)
+                mix(q, 1, g, [(0, True), (3, False)], [(3, mixed)])
+
+            @pl.when(me_z >= 2)
+            def _():
+                send_home(q, 1, g)
 
     @pl.loop(0, nq)
     def _(q):
         for g in range(ng):
             for peer in others_b:
                 to_basis(q, g, peer).wait_send()
-                home_in(q, g, peer).wait_send()
+                home_in(q, g, peer).wait()
+            keep(q, 0, g, 0).wait()
 
             @pl.when(me_z == 0)
             def _():
@@ -711,6 +700,24 @@
                 "state",
                 peer,
             ).wait_send()
+
+
+def place_kernel(group, home, o_ref):
+    nq, pair, _, packed = home.shape
+    ns = o_ref.shape[0]
+    cols = packed // ns
+    for b in range(pair):
+        for q in range(nq):
+            lane = (b * nq + q) * cols
+            for at, n, _ in lane_groups(cols, group):
+                full = n - n % LANES
+                for s in range(ns):
+                    src = ns * at + s * full
+                    to = lane + at
+                    o_ref[s, :, to : to + full] = home[q, b, :, src : src + full]
+                    if n % LANES:
+                        src = ns * (at + full) + s * (n - full)
+                        o_ref[s, :, to + full : to + n] = home[q, b, :, src : src + n - full]
 
 
 def fast_body(
@@ -738,11 +745,11 @@
     dma = pltpu.SemaphoreType.DMA
     vmem = pl.BlockSpec(memory_space=pltpu.VMEM)
     panel = (nq, 2, rows, lev, ns * cols)
-    return pl.pallas_call(
+    home = pl.pallas_call(
         functools.partial(step_kernel, nz, nb),
         in_specs=[pl.BlockSpec(memory_space=pl.ANY)] + [vmem] * 6,
-        out_specs=vmem,
-        out_shape=jax.ShapeDtypeStruct((ns, lev, joint), f32),
+        out_specs=pl.BlockSpec(memory_space=pl.ANY),
+        out_shape=jax.ShapeDtypeStruct((nq, nb, lev, ns * cols), f32),
         scratch_shapes=[
             pltpu.VMEM((ns, lev, joint), f32),
             pltpu.VMEM((m * lev, m * lev), bf16),
@@ -762,7 +769,6 @@
             pltpu.VMEM((total * total, lev, LANES), f32),
             pltpu.VMEM(panel, f32),
             pltpu.VMEM(panel, f32),
-            pltpu.VMEM((nq, nb, lev, ns * cols), f32),
             dma((ns, nq)),
         ]
         + [dma((nq, ng, nb))] * 2
@@ -782,6 +788,13 @@
         cavity_back,
         membrane_back,
     )
+    return pl.pallas_call(
+        functools.partial(place_kernel, group),
+        grid=(nb // PLACED,),
+        in_specs=[pl.BlockSpec((nq, PLACED, lev, ns * cols), lambda i: (0, i, 0, 0))],
+        out_specs=pl.BlockSpec((ns, lev, PLACED * nq * cols), lambda i: (0, 0, i)),
+        out_shape=jax.ShapeDtypeStruct((ns, lev, joint), f32),
+    )(home)
 
 
 def solution(mesh):

time: 212 us -> 210 us (level)
  local copies, waits for them, and re-layouts: 4.4 us -> 0 us
    pallas_call x0 -> x1, Pallas kernels: none -> 4.93 us  [fast_body(): pl.pallas_call(functools.partial(place_kernel, group), grid=(nb // PLACED...]
    unnamed x1 -> x0, local copies, waits for them, and re-layouts: 4.4 us -> none
    pallas_call x1, Pallas kernels: 207 us -> 204 us  [fast_body(): pl.pallas_call(functools.partial(step_kernel, nz, nb), in_specs=[pl.Block...]
where the time goes in v3:
time: 210 us; the launch traced here: 209 us
  Pallas kernels  209 us (100%)
    pallas_call x1, Pallas kernels, fast_body(): pl.pallas_call(functools.partial(step_kernel, nz, nb), in_specs=[pl.Block...  204 us
    pallas_call x1, Pallas kernels, fast_body(): pl.pallas_call(functools.partial(place_kernel, group), grid=(nb // PLACED...  4.93 us

profile of v3, /device:TPU:25, one launch (start us, length us, event | category | flops | bytes accessed | tf_op | source)
XLA Modules:
  0.0 209.4 jit_solution(7692591044045310436)
XLA Ops:
  0.0 204.4 %shard_map.73.home = f32[5,8,8,3200]{3,2,1,0:T(8,128)} custom-call(f32[2,8,64000]{2,1,0:T(8,128)} %x_ref.1, f32[40,40]{1,0:T(8,128)} %ms_ref.1, f32[64,64]{1,0:T(8,128)} %fc_ref.1, f32[40,64]{1,0:T(8,128)} %bitcast.1, f32[40,40]{1,0:T(8,128)} %fk_ref.1, f32[64,64]{1,0:T(8,128)} %bc_ref.1, f32[40,40]{1,0:T(8,128)} %bk_ref.1), custom_call_target="tpu_custom_call" | custom-call | tf_op jit(solution)/shard_map/pallas_call | solution.py:748
  204.4 4.9 %shard_map.74 = f32[2,8,64000]{2,1,0:T(8,128)} custom-call(f32[5,8,8,3200]{3,2,1,0:T(8,128)} %shard_map.73.home), custom_call_target="tpu_custom_call" | custom-call | tf_op jit(solution)/shard_map/pallas_call | solution.py:791
